TPU v7x, 256 devices: a whole 4x4x8 slice. The times are simulated.
256 devices in a mesh: expert: 32 (over z, x), col: 8 (over y, core).
Axes of the slice: x: 4, y: 4, z: 8, core: 2. Of those that a mesh axis runs over, the one named last changes fastest.
Arguments:
- tokens: bfloat16 [4096, 4096], P('expert', 'col'), may hold values from -6 to 6
- routes: int32 [4096, 8], P('expert'), may hold values from 0 to 63, all different within a row; in each aligned block of 128 rows (0 to 127, 128 to 255, ...) at most 24 rows name the same one
- route_weight: float32 [4096, 8], P('expert'), may hold values from 0.02 to 0.25
- language: int32 [4096], P('expert'), may hold values from 0 to 118
- lang_weight: float32 [119], replicated, may hold values from 0.01 to 0.1
- w_gate: bfloat16 [64, 1536, 4096], P('expert', 'col'), may hold values from -0.09375 to 0.09375
- w_up: bfloat16 [64, 1536, 4096], P('expert', 'col'), may hold values from -0.09375 to 0.09375
- w_down: bfloat16 [64, 1536, 4096], P('expert', None, 'col'), may hold values from -0.15625 to 0.15625
Outputs:
- layer_out: bfloat16 [4096, 4096], P('expert', 'col')
- gram: float32 [64, 1536, 1536], P('expert', 'col')
Inputs may be any that keep to these rules, and one draw needn't show every extreme that they name: `routes`: each row names 8 different experts. In each aligned block of 128 rows no expert is named by more than 24 rows, a bound that some block reaches.
All inputs are finite; a program needn't handle non-finite values.
Results may differ from a plain program's by a relative error of at most 0.0063.
Values may be sent and summed in bfloat16 or wider, within the bound.
A program may use at most 128 MiB of HBM per device.

v0:
```python
import jax
import jax.numpy as jnp
from jax import lax
from jax.sharding import PartitionSpec as P


def on_device(tokens, routes, route_weight, language, lang_weight, w_gate, w_up, w_down):
    tok_rows = routes.shape[0]
    top_count = routes.shape[1]
    local_exp = w_gate.shape[0]
    owners = lax.axis_size("expert")
    experts = local_exp * owners
    capacity = tok_rows * top_count * 3 // (2 * experts)
    expert_ids = jnp.arange(experts, dtype=jnp.int32)
    chosen = routes[:, :, None] == expert_ids[None, None, :]
    hits = jnp.any(chosen, axis=1).astype(jnp.int32)
    coefs = jnp.sum(jnp.where(chosen, route_weight[:, :, None], jnp.zeros((), jnp.float32)), axis=1)
    places = jnp.cumsum(hits, axis=0) - hits
    slot_ids = jnp.arange(capacity, dtype=jnp.int32)
    picks = (hits.T[:, None, :] == 1) & (places.T[:, None, :] == slot_ids[None, :, None])
    row_index = jnp.arange(tok_rows, dtype=jnp.int32)
    slot_token = jnp.sum(jnp.where(picks, row_index[None, None, :], 0), axis=2)
    filled = jnp.any(picks, axis=2)
    lang_table = language[:, None] == jnp.arange(lang_weight.shape[0], dtype=jnp.int32)[None, :]
    calib = jnp.sum(
        jnp.where(lang_table, lang_weight[None, :], jnp.zeros((), jnp.float32)), axis=1
    ).astype(jnp.bfloat16)
    slot_cal = jnp.where(filled, calib[slot_token], jnp.zeros((), jnp.bfloat16)).reshape(
        owners, local_exp, capacity
    )
    slot_coef = jnp.where(
        filled, jnp.take_along_axis(coefs.T, slot_token, axis=1), jnp.zeros((), jnp.float32)
    )
    flat_token = slot_token.reshape(-1)
    flat_filled = filled.reshape(-1)
    whole = lax.all_gather(tokens, "col", axis=1, tiled=True)
    rows = jnp.take(whole, flat_token, axis=0)
    rows = jnp.where(flat_filled[:, None], rows, jnp.zeros((), jnp.bfloat16))
    arrived = lax.all_to_all(
        rows.reshape(owners, local_exp, capacity, whole.shape[1]),
        "expert",
        split_axis=0,
        concat_axis=0,
        tiled=True,
    )
    arrived_cal = lax.all_to_all(slot_cal, "expert", split_axis=0, concat_axis=0, tiled=True)
    gate = jnp.einsum("seck,efk->escf", arrived, w_gate, preferred_element_type=jnp.float32)
    upper = jnp.einsum("seck,efk->escf", arrived, w_up, preferred_element_type=jnp.float32)
    hidden = (jax.nn.silu(gate) * upper).astype(jnp.bfloat16)
    cal_rows = jnp.transpose(arrived_cal, (1, 0, 2))
    scaled = (cal_rows[..., None].astype(jnp.float32) * hidden.astype(jnp.float32)).astype(
        jnp.bfloat16
    )
    d_local = w_down.shape[2]
    piece = lax.all_gather(hidden, "col", axis=3, tiled=True)
    block = jnp.einsum("escu,escv->euv", scaled, piece, preferred_element_type=jnp.float32)
    mixed_now = jnp.einsum("escv,evd->escd", piece, w_down, preferred_element_type=jnp.float32)
    expert_out = mixed_now.astype(jnp.bfloat16)
    returned = lax.all_to_all(expert_out, "expert", split_axis=1, concat_axis=0, tiled=True)
    returned = returned.reshape(experts * capacity, d_local).astype(jnp.float32)
    combined = jnp.zeros((tok_rows, d_local), jnp.float32)
    combined = combined.at[flat_token].add(slot_coef.reshape(-1)[:, None] * returned)
    return (combined.astype(jnp.bfloat16), block)


def solution(mesh):
    in_specs = (
        P("expert", "col"),
        P("expert", None),
        P("expert", None),
        P("expert"),
        P(),
        P("expert", "col", None),
        P("expert", "col", None),
        P("expert", None, "col"),
    )
    out_specs = (P("expert", "col"), P("expert", "col", None))
    return jax.shard_map(
        on_device, mesh=mesh, in_specs=in_specs, out_specs=out_specs, check_vma=False
    )
```

profile of v0, /device:TPU:4, one launch (start us, length us, event | category | flops | bytes accessed | tf_op | source)
XLA Modules:
  0.0 570.8 jit_solution(8276990550696766480)
XLA Ops:
  7.2 0.7 all-gather.3.cloned.1.call-update
  8.0 0.9 fusion.18
  9.3 1.2 select_reduce_fusion
  10.6 1.2 fusion.17
  11.9 26.8 %all-gather.3.cloned.1.call-done = bf16[128,4096]{1,0:T(8,128)(2,1)} async-done(((bf16[128,512]{1,0:T(8,128)(2,1)}), bf16[128,4096]{1,0:T(8,128)(2,1)}) %all-gather.3.cloned.1.call-update) | async-done | bytes 1048592 | tf_op jit(solution)/shard_map/all_gather | solution.py:36
  38.8 23.4 %gather_fusion = bf16[1536,4096]{1,0:T(8,128)(2,1)} fusion(bf16[128,4096]{1,0:T(8,128)(2,1)} %all-gather.3.cloned.1.call-done, s32[2048]{0:T(1024)S(1)} %pad_clamp_fusion.1), kind=kCustom, calls=%fused_computation | custom fusion | bytes 25171968 | tf_op jit(solution)/shard_map/jit(_take)/gather | solution.py:37
  62.2 6.7 %select_select_fusion = bf16[32,2,24,4096]{3,2,1,0:T(8,128)(2,1)S(1)} fusion(bf16[32,2,24,4096]{3,2,1,0:T(8,128)(2,1)} %bitcast.49, pred[32,2,24]{2,1,0:T(4,128)(4,1)S(1)} %compare_and_fusion, pred[32,2,24]{2,1,0:T(4,128)(4,1)S(1)} %broadcast_in_dim.95), kind=kLoop, calls=%fused_computation.4 | loop fusion | flops 12582912 | bytes 25168896 | tf_op jit(solution)/shard_map/jit(_where)/select_n | solution.py:38
  68.9 285.7 %all_to_all.19 = bf16[32,2,24,4096]{3,2,1,0:T(8,128)(2,1)} all-to-all(bf16[32,2,24,4096]{3,2,1,0:T(8,128)(2,1)S(1)} %select_select_fusion), channel_id=1, replica_groups=mesh['expert'=32,'col'=8] {'expert'}, dimensions={0} | all-to-all | bytes 25165824 | tf_op jit(solution)/shard_map/all_to_all | solution.py:39
  354.6 10.1 %fusion.2 = f32[2,32,24,192]{3,2,1,0:T(8,128)} fusion(bf16[32,2,24,4096]{3,2,1,0:T(8,128)(2,1)} %all_to_all.19, bf16[2,192,4096]{2,1,0:T(8,128)(2,1)} %param.13), kind=kOutput, calls=%fused_computation.7 | convolution fusion | flops 2415919104 | bytes 16908288 | tf_op jit(solution)/shard_map/seck,efk->escf/dot_general | solution.py:47
  364.7 10.5 %multiply_convert_fusion.1 = bf16[2,32,24,192]{3,2,1,0:T(8,128)(2,1)} fusion(f32[2,32,24,192]{3,2,1,0:T(8,128)} %fusion.2, bf16[2,192,4096]{2,1,0:T(8,128)(2,1)} %param.14, bf16[32,2,24,4096]{3,2,1,0:T(8,128)(2,1)} %all_to_all.19), kind=kOutput, calls=%fused_computation.18 | convolution fusion | flops 2417688576 | bytes 17498112 | tf_op jit(solution)/shard_map/seck,efk->escf/dot_general | solution.py:48
  375.1 3.7 copy.44
  379.1 9.0 %gather_fusion.1 = bf16[1536]{0:T(1024)(128)(2,1)S(1)} fusion(bf16[128]{0:T(256)(128)(2,1)S(1)} %select_reduce_fusion.2, s32[2048]{0:T(1024)S(1)} %pad_clamp_fusion), kind=kCustom, calls=%fused_computation.1 | custom fusion | bytes 12288 | tf_op jit(solution)/shard_map/gather | solution.py:28
  388.8 5.5 all-to-all-start.2
  394.4 76.2 %all-gather.5.cloned.1.call-done = bf16[2,32,24,1536]{1,2,0,3:T(8,128)(2,1)} async-done(((bf16[2,32,24,192]{1,2,0,3:T(8,128)(2,1)}), bf16[2,32,24,1536]{1,2,0,3:T(8,128)(2,1)}) %all-gather.5.cloned.1.call-update) | async-done | bytes 4718608 | tf_op jit(solution)/shard_map/all_gather | solution.py:55
  470.6 22.1 %copy.45 = bf16[2,32,24,1536]{3,2,1,0:T(8,128)(2,1)} copy(bf16[2,32,24,1536]{1,2,0,3:T(8,128)(2,1)} %all-gather.5.cloned.1.call-done) | data formatting | bytes 9437184 | tf_op jit(solution)/shard_map/all_gather | solution.py:55
  492.7 5.0 fusion.8
  497.8 1.3 copy.46
  499.1 10.2 %all-to-all-start.1 = ((bf16[2,32,24,512]{3,2,0,1:T(8,128)(2,1)}), bf16[2,32,24,512]{3,2,0,1:T(8,128)(2,1)}, u32[]{:S(2)}, u32[]{:S(2)}) async-start(bf16[2,32,24,512]{3,2,0,1:T(8,128)(2,1)} %copy.46), calls=%async_computation.1 | async-start | bytes 3145728 | tf_op jit(solution)/shard_map/all_to_all | solution.py:59
  509.7 10.7 %gather_fusion.2 = f32[1536]{0:T(1024)S(1)} fusion(f32[64,128]{0,1:T(8,128)S(1)} %bitcast.48, s32[1536]{0:T(1024)S(1)} %reshape.137), kind=kCustom, calls=%fused_computation.2 | custom fusion | bytes 24576 | tf_op jit(solution)/shard_map/jit(take_along_axis)/gather | solution.py:32
  520.5 5.2 convolution_bitcast_fusion
  525.6 23.4 %all-to-all-done.1 = bf16[2,32,24,512]{3,2,0,1:T(8,128)(2,1)} async-done(((bf16[2,32,24,512]{3,2,0,1:T(8,128)(2,1)}), bf16[2,32,24,512]{3,2,0,1:T(8,128)(2,1)}, u32[]{:S(2)}, u32[]{:S(2)}) %all-to-all-start.1) | async-done | bytes 1572896 | tf_op jit(solution)/shard_map/all_to_all | solution.py:59
  549.1 1.8 bitcast_convert_fusion
  550.9 1.9 bitcast_multiply_fusion
  552.8 10.4 %scatter_custom_fusion = f32[128,512]{1,0:T(8,128)S(1)} fusion(s32[1536]{0:T(1024)S(1)} %fusion.21, f32[1536,512]{1,0:T(8,128)} %bitcast_multiply_fusion, f32[]{:T(128)} %constant.16.clone.1), kind=kCustom, calls=%fused_computation.27 | custom fusion | flops 786432 | bytes 262656 | tf_op jit(solution)/shard_map/scatter-add | solution.py:62
  (40 shorter events, 2.8 us)
Async XLA Ops:
  7.2 485.5 %copy-start = (bf16[2,1536,512]{2,1,0:T(8,128)(2,1)S(1)}, bf16[2,1536,512]{2,1,0:T(8,128)(2,1)}, u32[]{:S(2)}) copy-start(bf16[2,1536,512]{2,1,0:T(8,128)(2,1)} %param.15) | copy-start | bytes 9437188
  7.2 31.6 %all-gather.3.cloned.1.call-start = ((), (), s32[]{:S(2)}) async-start(), calls=%async_computation.3 | async-start | bytes 1179648 | tf_op jit(solution)/shard_map/all_gather | solution.py:36
  7.9 462.7 %all-gather.5.cloned.1.call-start = ((), (), s32[]{:S(2)}) async-start(), calls=%async_computation.4 | async-start | bytes 21233664 | tf_op jit(solution)/shard_map/all_gather | solution.py:55
  375.1 3.8 copy-start.3
  375.1 3.8 copy-start.4
  388.8 110.2 %all-to-all-start.2 = ((bf16[32,2,24]{2,1,0:T(2,128)(2,1)}), bf16[32,2,24]{2,1,0:T(2,128)(2,1)S(1)}, u32[]{:S(2)}, u32[]{:S(2)}) async-start(bf16[32,2,24]{2,1,0:T(2,128)(2,1)} %broadcast_select_fusion), calls=%async_computation.2 | async-start | bytes 32768 | tf_op jit(solution)/shard_map/all_to_all | solution.py:46
  497.7 11.7 %copy-start.1 = (s32[128,8]{0,1:T(8,128)S(1)}, s32[128,8]{0,1:T(8,128)}, u32[]{:S(2)}) copy-start(s32[128,8]{0,1:T(8,128)} %param.9) | copy-start | bytes 12292
  497.7 11.7 %copy-start.2 = (f32[128,8]{0,1:T(8,128)S(1)}, f32[128,8]{0,1:T(8,128)}, u32[]{:S(2)}) copy-start(f32[128,8]{0,1:T(8,128)} %param.10) | copy-start | bytes 12292
  499.1 50.0 %all-to-all-start.1 = ((bf16[2,32,24,512]{3,2,0,1:T(8,128)(2,1)}), bf16[2,32,24,512]{3,2,0,1:T(8,128)(2,1)}, u32[]{:S(2)}, u32[]{:S(2)}) async-start(bf16[2,32,24,512]{3,2,0,1:T(8,128)(2,1)} %copy.46), calls=%async_computation.1 | async-start | bytes 3145728 | tf_op jit(solution)/shard_map/all_to_all | solution.py:59
Sparse Core Ops, SparseCore 0:
  9.8 28.8 all-gather.2
  379.0 91.6 all-gather.4
where the time goes:
time: 572 us; the launch traced here: 571 us
  blocking collectives  286 us (50%)
  waiting for transfers between devices  127 us (22%)
  local copies, waits for them, and re-layouts  71.1 us (12%)
  matrix products  30.7 us (5%)
  other arithmetic  25.9 us (5%)
  starting transfers between devices  15.8 us (3%)
  between operations  14.3 us (2%)
    all_to_all x1, blocking collectives, on_device(): lax.all_to_all(rows.reshape(owners, local_exp, capacity, whole.shape[1]),...  286 us
    all_gather x1, waiting for transfers between devices, on_device(): piece = lax.all_gather(hidden, 'col', axis=3, tiled=True)  76.2 us
    all_gather x1, waiting for transfers between devices, on_device(): whole = lax.all_gather(tokens, 'col', axis=1, tiled=True)  26.8 us
    all_to_all x1, waiting for transfers between devices, on_device(): lax.all_to_all(expert_out, 'expert', split_axis=1, concat_axis=0, tiled=T...  23.4 us
    gather x1, local copies, waits for them, and re-layouts, on_device(): rows = jnp.take(whole, flat_token, axis=0)  23.4 us
    all_gather x1, local copies, waits for them, and re-layouts, on_device(): piece = lax.all_gather(hidden, 'col', axis=3, tiled=True)  22.1 us
  transfers between devices with their start and end apart: 4, of which 3 were waited for; matrix products, arithmetic and copies ran while one was open for 10% of the time, Pallas kernels for 0%

commit v1 on v0

--- a/solution.py
+++ b/solution.py
@@ -52,7 +52,21 @@
         jnp.bfloat16
     )
     d_local = w_down.shape[2]
-    piece = lax.all_gather(hidden, "col", axis=3, tiled=True)
+    ways, here, step = (lax.axis_size("col"), lax.axis_index("col"), hidden.shape[3])
+    dims = [n * ways if d == 3 else n for d, n in enumerate(hidden.shape)]
+    full = lax.dynamic_update_slice_in_dim(
+        jnp.zeros(dims, hidden.dtype), hidden, here * step, axis=3
+    )
+    going_up = going_down = hidden
+    for far in range(1, ways // 2 + 1):
+        going_up = lax.ppermute(going_up, "col", [(d, (d + 1) % ways) for d in range(ways)])
+        full = lax.dynamic_update_slice_in_dim(full, going_up, (here - far) % ways * step, axis=3)
+        if 2 * far < ways:
+            going_down = lax.ppermute(going_down, "col", [(d, (d - 1) % ways) for d in range(ways)])
+            full = lax.dynamic_update_slice_in_dim(
+                full, going_down, (here + far) % ways * step, axis=3
+            )
+    piece = full
     block = jnp.einsum("escu,escv->euv", scaled, piece, preferred_element_type=jnp.float32)
     mixed_now = jnp.einsum("escv,evd->escd", piece, w_down, preferred_element_type=jnp.float32)
     expert_out = mixed_now.astype(jnp.bfloat16)

time: 572 us -> 600 us (1.049)
  local copies, waits for them, and re-layouts: 71.1 us -> 141 us
  waiting for transfers between devices: 127 us -> 75.6 us
  starting transfers between devices: 15.8 us -> 23.5 us
    dynamic_update_slice x0 -> x8, local copies, waits for them, and re-layouts: none -> 91 us  [the longest x4 45.1 us: on_device(): lax.dynamic_update_slice_in_dim(full, going_up, (here - far) % ways * ste...]
    all_gather x1 -> x0, waiting for transfers between devices: 76.2 us -> none  [on_device(): piece = lax.all_gather(hidden, 'col', axis=3, tiled=True)]
    ppermute x0 -> x7, waiting for transfers between devices: none -> 29.2 us  [the longest x4 29.2 us: on_device(): lax.ppermute(going_up, 'col', [(d, (d + 1) % ways) for d in range(ways)])]
    all_gather x1 -> x0, local copies, waits for them, and re-layouts: 22.1 us -> none  [on_device(): piece = lax.all_gather(hidden, 'col', axis=3, tiled=True)]
    ppermute x0 -> x7, starting transfers between devices: none -> 8.02 us  [the longest x3 8.01 us: on_device(): lax.ppermute(going_down, 'col', [(d, (d - 1) % ways) for d in range(ways)])]
  transfers between devices with their start and end apart: 4 -> 10, of which waited for: 3 -> 5; matrix products, arithmetic and copies ran while one was open for 10% -> 22% of each run, Pallas kernels for 0% -> 0%
where the time goes in v1:
time: 600 us; the launch traced here: 597 us
  blocking collectives  286 us (48%)
  local copies, waits for them, and re-layouts  141 us (24%)
  waiting for transfers between devices  75.6 us (13%)
  matrix products  30.7 us (5%)
  other arithmetic  25.9 us (4%)
  starting transfers between devices  23.5 us (4%)
  between operations  14.4 us (2%)
    all_to_all x1, blocking collectives, on_device(): lax.all_to_all(rows.reshape(owners, local_exp, capacity, whole.shape[1]),...  286 us
    dynamic_update_slice x4, local copies, waits for them, and re-layouts, on_device(): lax.dynamic_update_slice_in_dim(full, going_up, (here - far) % ways * ste...  45.1 us
    dynamic_update_slice x3, local copies, waits for them, and re-layouts, on_device(): lax.dynamic_update_slice_in_dim(full, going_down, (here + far) % ways * s...  37.1 us
    ppermute x4, waiting for transfers between devices, on_device(): lax.ppermute(going_up, 'col', [(d, (d + 1) % ways) for d in range(ways)])  29.2 us
    all_gather x1, waiting for transfers between devices, on_device(): whole = lax.all_gather(tokens, 'col', axis=1, tiled=True)  26.8 us
    gather x1, local copies, waits for them, and re-layouts, on_device(): rows = jnp.take(whole, flat_token, axis=0)  23.4 us
    all_to_all x1, waiting for transfers between devices, on_device(): lax.all_to_all(expert_out, 'expert', split_axis=1, concat_axis=0, tiled=T...  18.9 us
  transfers between devices with their start and end apart: 10, of which 5 were waited for; matrix products, arithmetic and copies ran while one was open for 22% of the time, Pallas kernels for 0%

profile of v1, /device:TPU:4, one launch (start us, length us, event | category | flops | bytes accessed | tf_op | source)
XLA Modules:
  0.0 596.6 jit_solution(10741539304051058633)
XLA Ops:
  11.9 26.8 %all-gather.2.cloned.1.call-done = bf16[128,4096]{1,0:T(8,128)(2,1)} async-done(((bf16[128,512]{1,0:T(8,128)(2,1)}), bf16[128,4096]{1,0:T(8,128)(2,1)}) %all-gather.2.cloned.1.call-update) | async-done | bytes 1048592 | tf_op jit(solution)/shard_map/all_gather | solution.py:36
  38.8 23.4 %gather_fusion = bf16[1536,4096]{1,0:T(8,128)(2,1)} fusion(bf16[128,4096]{1,0:T(8,128)(2,1)} %all-gather.2.cloned.1.call-done, s32[2048]{0:T(1024)S(1)} %pad_clamp_fusion.1), kind=kCustom, calls=%fused_computation | custom fusion | bytes 25171968 | tf_op jit(solution)/shard_map/jit(_take)/gather | solution.py:37
  62.2 6.7 %select_select_fusion = bf16[32,2,24,4096]{3,2,1,0:T(8,128)(2,1)S(1)} fusion(bf16[32,2,24,4096]{3,2,1,0:T(8,128)(2,1)} %bitcast.49, pred[32,2,24]{2,1,0:T(4,128)(4,1)S(1)} %compare_and_fusion, pred[32,2,24]{2,1,0:T(4,128)(4,1)S(1)} %broadcast_in_dim.99), kind=kLoop, calls=%fused_computation.4 | loop fusion | flops 12582912 | bytes 25168896 | tf_op jit(solution)/shard_map/jit(_where)/select_n | solution.py:38
  68.9 285.7 %all_to_all.19 = bf16[32,2,24,4096]{3,2,1,0:T(8,128)(2,1)} all-to-all(bf16[32,2,24,4096]{3,2,1,0:T(8,128)(2,1)S(1)} %select_select_fusion), channel_id=1, replica_groups=mesh['expert'=32,'col'=8] {'expert'}, dimensions={0} | all-to-all | bytes 25165824 | tf_op jit(solution)/shard_map/all_to_all | solution.py:39
  354.6 10.0 %fusion.2 = f32[2,32,24,192]{3,2,1,0:T(8,128)} fusion(bf16[32,2,24,4096]{3,2,1,0:T(8,128)(2,1)} %all_to_all.19, bf16[2,192,4096]{2,1,0:T(8,128)(2,1)} %param.13), kind=kOutput, calls=%fused_computation.7 | convolution fusion | flops 2415919104 | bytes 16908288 | tf_op jit(solution)/shard_map/seck,efk->escf/dot_general | solution.py:47
  364.7 10.5 %multiply_convert_fusion.1 = bf16[2,32,24,192]{3,2,1,0:T(8,128)(2,1)} fusion(f32[2,32,24,192]{3,2,1,0:T(8,128)} %fusion.2, bf16[2,192,4096]{2,1,0:T(8,128)(2,1)} %param.14, bf16[32,2,24,4096]{3,2,1,0:T(8,128)(2,1)} %all_to_all.19), kind=kOutput, calls=%fused_computation.18 | convolution fusion | flops 2417688576 | bytes 17498112 | tf_op jit(solution)/shard_map/seck,efk->escf/dot_general | solution.py:48
  378.2 9.9 %collective-permute-done = bf16[2,32,24,192]{3,2,1,0:T(8,128)(2,1)S(1)} collective-permute-done((bf16[2,32,24,192]{3,2,1,0:T(8,128)(2,1)}, bf16[2,32,24,192]{3,2,1,0:T(8,128)(2,1)S(1)}, u32[]{:S(2)}, u32[]{:S(2)}) %collective-permute-start) | collective-permute-done | bytes 589856 | tf_op jit(solution)/shard_map/ppermute | solution.py:62
  391.9 9.7 %collective-permute-done.2 = bf16[2,32,24,192]{3,2,1,0:T(8,128)(2,1)S(1)} collective-permute-done((bf16[2,32,24,192]{3,2,1,0:T(8,128)(2,1)S(1)}, bf16[2,32,24,192]{3,2,1,0:T(8,128)(2,1)S(1)}, u32[]{:S(2)}, u32[]{:S(2)}) %collective-permute-start.2) | collective-permute-done | bytes 589856 | tf_op jit(solution)/shard_map/ppermute | solution.py:62
  404.6 9.7 %collective-permute-done.4 = bf16[2,32,24,192]{3,2,1,0:T(8,128)(2,1)} collective-permute-done((bf16[2,32,24,192]{3,2,1,0:T(8,128)(2,1)S(1)}, bf16[2,32,24,192]{3,2,1,0:T(8,128)(2,1)}, u32[]{:S(2)}, u32[]{:S(2)}) %collective-permute-start.4) | collective-permute-done | bytes 589856 | tf_op jit(solution)/shard_map/ppermute | solution.py:62
  414.5 9.0 %gather_fusion.1 = bf16[1536]{0:T(1024)(128)(2,1)S(1)} fusion(bf16[128]{0:T(256)(128)(2,1)S(1)} %select_reduce_fusion.2, s32[2048]{0:T(1024)S(1)} %pad_clamp_fusion), kind=kCustom, calls=%fused_computation.1 | custom fusion | bytes 12288 | tf_op jit(solution)/shard_map/gather | solution.py:28
  424.3 5.6 all-to-all-start.2
  432.4 8.8 %dynamic_update_slice.24 = bf16[2,32,24,1536]{3,2,1,0:T(8,128)(2,1)} dynamic-update-slice(bf16[2,32,24,1536]{3,2,1,0:T(8,128)(2,1)} %broadcast_in_dim.98, bf16[2,32,24,192]{3,2,1,0:T(8,128)(2,1)} %multiply_convert_fusion.1, s32[]{:T(128)} %constant.90.clone.1, s32[]{:T(128)} %constant.90.clone.1, s32[]{:T(128)} %constant.90.clone.1, s32[]{:T(128)S(6)} %select_n.145) | dynamic-update-slice | bytes 1179652 | tf_op jit(solution)/shard_map/dynamic_update_slice | solution.py:57
  441.2 13.5 %dynamic_update_slice.25 = bf16[2,32,24,1536]{3,2,1,0:T(8,128)(2,1)} dynamic-update-slice(bf16[2,32,24,1536]{3,2,1,0:T(8,128)(2,1)} %dynamic_update_slice.24, bf16[2,32,24,192]{3,2,1,0:T(8,128)(2,1)} %copy-done.1, s32[]{:T(128)} %constant.90.clone.1, s32[]{:T(128)} %constant.90.clone.1, s32[]{:T(128)} %constant.90.clone.1, s32[]{:T(128)S(6)} %select_n.147) | dynamic-update-slice | bytes 1179652 | tf_op jit(solution)/shard_map/dynamic_update_slice | solution.py:63
  454.7 14.2 %dynamic_update_slice.26 = bf16[2,32,24,1536]{3,2,1,0:T(8,128)(2,1)} dynamic-update-slice(bf16[2,32,24,1536]{3,2,1,0:T(8,128)(2,1)} %dynamic_update_slice.25, bf16[2,32,24,192]{3,2,1,0:T(8,128)(2,1)} %copy-done.2, s32[]{:T(128)} %constant.90.clone.1, s32[]{:T(128)} %constant.90.clone.1, s32[]{:T(128)} %constant.90.clone.1, s32[]{:T(128)S(6)} %select_n.149) | dynamic-update-slice | bytes 1179652 | tf_op jit(solution)/shard_map/dynamic_update_slice | solution.py:66
  468.9 8.7 %dynamic_update_slice.27 = bf16[2,32,24,1536]{3,2,1,0:T(8,128)(2,1)} dynamic-update-slice(bf16[2,32,24,1536]{3,2,1,0:T(8,128)(2,1)} %dynamic_update_slice.26, bf16[2,32,24,192]{3,2,1,0:T(8,128)(2,1)} %copy-done.3, s32[]{:T(128)} %constant.90.clone.1, s32[]{:T(128)} %constant.90.clone.1, s32[]{:T(128)} %constant.90.clone.1, s32[]{:T(128)S(6)} %select_n.151) | dynamic-update-slice | bytes 1179652 | tf_op jit(solution)/shard_map/dynamic_update_slice | solution.py:63
  477.5 8.8 %dynamic_update_slice.28 = bf16[2,32,24,1536]{3,2,1,0:T(8,128)(2,1)} dynamic-update-slice(bf16[2,32,24,1536]{3,2,1,0:T(8,128)(2,1)} %dynamic_update_slice.27, bf16[2,32,24,192]{3,2,1,0:T(8,128)(2,1)} %collective-permute-done.3, s32[]{:T(128)} %constant.90.clone.1, s32[]{:T(128)} %constant.90.clone.1, s32[]{:T(128)} %constant.90.clone.1, s32[]{:T(128)S(6)} %select_n.153) | dynamic-update-slice | bytes 1179652 | tf_op jit(solution)/shard_map/dynamic_update_slice | solution.py:66
  486.3 14.1 %dynamic_update_slice.29 = bf16[2,32,24,1536]{3,2,1,0:T(8,128)(2,1)} dynamic-update-slice(bf16[2,32,24,1536]{3,2,1,0:T(8,128)(2,1)} %dynamic_update_slice.28, bf16[2,32,24,192]{3,2,1,0:T(8,128)(2,1)} %collective-permute-done.4, s32[]{:T(128)} %constant.90.clone.1, s32[]{:T(128)} %constant.90.clone.1, s32[]{:T(128)} %constant.90.clone.1, s32[]{:T(128)S(6)} %select_n.155) | dynamic-update-slice | bytes 1179652 | tf_op jit(solution)/shard_map/dynamic_update_slice | solution.py:63
  500.4 14.2 %dynamic_update_slice.30 = bf16[2,32,24,1536]{3,2,1,0:T(8,128)(2,1)} dynamic-update-slice(bf16[2,32,24,1536]{3,2,1,0:T(8,128)(2,1)} %dynamic_update_slice.29, bf16[2,32,24,192]{3,2,1,0:T(8,128)(2,1)} %collective-permute-done.5, s32[]{:T(128)} %constant.90.clone.1, s32[]{:T(128)} %constant.90.clone.1, s32[]{:T(128)} %constant.90.clone.1, s32[]{:T(128)S(6)} %select_n.157) | dynamic-update-slice | bytes 1179652 | tf_op jit(solution)/shard_map/dynamic_update_slice | solution.py:66
  514.6 8.8 %dynamic_update_slice.31 = bf16[2,32,24,1536]{3,2,1,0:T(8,128)(2,1)} dynamic-update-slice(bf16[2,32,24,1536]{3,2,1,0:T(8,128)(2,1)} %dynamic_update_slice.30, bf16[2,32,24,192]{3,2,1,0:T(8,128)(2,1)} %collective-permute-done.6, s32[]{:T(128)} %constant.90.clone.1, s32[]{:T(128)} %constant.90.clone.1, s32[]{:T(128)} %constant.90.clone.1, s32[]{:T(128)S(6)} %select_n.159) | dynamic-update-slice | bytes 1179652 | tf_op jit(solution)/shard_map/dynamic_update_slice | solution.py:63
  529.8 9.8 %all-to-all-start.1 = ((bf16[2,32,24,512]{3,2,0,1:T(8,128)(2,1)}), bf16[2,32,24,512]{3,2,0,1:T(8,128)(2,1)}, u32[]{:S(2)}, u32[]{:S(2)}) async-start(bf16[2,32,24,512]{3,2,0,1:T(8,128)(2,1)} %copy.57), calls=%async_computation.1 | async-start | bytes 3145728 | tf_op jit(solution)/shard_map/all_to_all | solution.py:73
  540.0 10.7 %gather_fusion.2 = f32[1536]{0:T(1024)S(1)} fusion(f32[64,128]{0,1:T(8,128)S(1)} %bitcast.48, s32[1536]{0:T(1024)S(1)} %reshape.137), kind=kCustom, calls=%fused_computation.2 | custom fusion | bytes 24576 | tf_op jit(solution)/shard_map/jit(take_along_axis)/gather | solution.py:32
  550.8 5.2 convolution_bitcast_fusion
  556.0 18.9 %all-to-all-done.1 = bf16[2,32,24,512]{3,2,0,1:T(8,128)(2,1)} async-done(((bf16[2,32,24,512]{3,2,0,1:T(8,128)(2,1)}), bf16[2,32,24,512]{3,2,0,1:T(8,128)(2,1)}, u32[]{:S(2)}, u32[]{:S(2)}) %all-to-all-start.1) | async-done | bytes 1572896 | tf_op jit(solution)/shard_map/all_to_all | solution.py:73
  578.6 10.4 %scatter_custom_fusion = f32[128,512]{1,0:T(8,128)S(1)} fusion(s32[1536]{0:T(1024)S(1)} %fusion.21, f32[1536,512]{1,0:T(8,128)} %bitcast_multiply_fusion, f32[]{:T(128)} %constant.87.clone.1), kind=kCustom, calls=%fused_computation.27 | custom fusion | flops 786432 | bytes 262656 | tf_op jit(solution)/shard_map/scatter-add | solution.py:76
  (64 shorter events, 29.1 us)
Async XLA Ops:
  7.2 516.2 %copy-start = (bf16[2,1536,512]{2,1,0:T(8,128)(2,1)S(1)}, bf16[2,1536,512]{2,1,0:T(8,128)(2,1)}, u32[]{:S(2)}) copy-start(bf16[2,1536,512]{2,1,0:T(8,128)(2,1)} %param.15) | copy-start | bytes 9437188
  7.2 31.6 %all-gather.2.cloned.1.call-start = ((), (), s32[]{:S(2)}) async-start(), calls=%async_computation.3 | async-start | bytes 1179648 | tf_op jit(solution)/shard_map/all_gather | solution.py:36
  364.7 49.7 %copy-start.6 = (f32[119]{0:T(128)S(1)}, f32[119]{0:T(128)}, u32[]{:S(2)}) copy-start(f32[119]{0:T(128)} %param.12) | copy-start | bytes 1432
  364.7 49.7 %copy-start.7 = (s32[128]{0:T(128)S(1)}, s32[128]{0:T(128)}, u32[]{:S(2)}) copy-start(s32[128]{0:T(128)} %param.11) | copy-start | bytes 1540
  375.2 12.8 %collective-permute-start = (bf16[2,32,24,192]{3,2,1,0:T(8,128)(2,1)}, bf16[2,32,24,192]{3,2,1,0:T(8,128)(2,1)S(1)}, u32[]{:S(2)}, u32[]{:S(2)}) collective-permute-start(bf16[2,32,24,192]{3,2,1,0:T(8,128)(2,1)} %multiply_convert_fusion.1), channel_id=1, source_target_pairs={{0,1},{1,2},{2,3},{3,4},{4,5},{5,6},{6,7},{7,0},{8,9},{9,10},{10,1... | collective-permute-start | bytes 1769480 | tf_op jit(solution)/shard_map/ppermute | solution.py:62
  375.2 13.7 %collective-permute-start.1 = (bf16[2,32,24,192]{3,2,1,0:T(8,128)(2,1)}, bf16[2,32,24,192]{3,2,1,0:T(8,128)(2,1)S(1)}, u32[]{:S(2)}, u32[]{:S(2)}) collective-permute-start(bf16[2,32,24,192]{3,2,1,0:T(8,128)(2,1)} %multiply_convert_fusion.1), channel_id=1, source_target_pairs={{0,7},{1,0},{2,1},{3,2},{4,3},{5,4},{6,5},{7,6},{8,15},{9,8},{10,9... | collective-permute-start | bytes 1769480 | tf_op jit(solution)/shard_map/ppermute | solution.py:65
  388.0 0.9 copy-start.1
  388.9 12.6 %collective-permute-start.2 = (bf16[2,32,24,192]{3,2,1,0:T(8,128)(2,1)S(1)}, bf16[2,32,24,192]{3,2,1,0:T(8,128)(2,1)S(1)}, u32[]{:S(2)}, u32[]{:S(2)}) collective-permute-start(bf16[2,32,24,192]{3,2,1,0:T(8,128)(2,1)S(1)} %collective-permute-done), channel_id=1, source_target_pairs={{0,1},{1,2},{2,3},{3,4},{4,5},{5,6},{6,7},{7,0},{8,9},{9,10},{10,1... | collective-permute-start | bytes 1769480 | tf_op jit(solution)/shard_map/ppermute | solution.py:62
  388.9 12.6 %copy-start.2 = (bf16[2,32,24,192]{3,2,1,0:T(8,128)(2,1)}, bf16[2,32,24,192]{3,2,1,0:T(8,128)(2,1)S(1)}, u32[]{:S(2)}) copy-start(bf16[2,32,24,192]{3,2,1,0:T(8,128)(2,1)S(1)} %collective-permute-done.1) | copy-start | bytes 1769476
  388.9 12.6 %collective-permute-start.3 = (bf16[2,32,24,192]{3,2,1,0:T(8,128)(2,1)S(1)}, bf16[2,32,24,192]{3,2,1,0:T(8,128)(2,1)}, u32[]{:S(2)}, u32[]{:S(2)}) collective-permute-start(bf16[2,32,24,192]{3,2,1,0:T(8,128)(2,1)S(1)} %collective-permute-done.1), channel_id=1, source_target_pairs={{0,7},{1,0},{2,1},{3,2},{4,3},{5,4},{6,5},{7,6},{8,15},{9,8},{10,9... | collective-permute-start | bytes 1769480 | tf_op jit(solution)/shard_map/ppermute | solution.py:65
  401.5 1.0 copy-start.3
  401.5 12.7 %collective-permute-start.4 = (bf16[2,32,24,192]{3,2,1,0:T(8,128)(2,1)S(1)}, bf16[2,32,24,192]{3,2,1,0:T(8,128)(2,1)}, u32[]{:S(2)}, u32[]{:S(2)}) collective-permute-start(bf16[2,32,24,192]{3,2,1,0:T(8,128)(2,1)S(1)} %collective-permute-done.2), channel_id=1, source_target_pairs={{0,1},{1,2},{2,3},{3,4},{4,5},{5,6},{6,7},{7,0},{8,9},{9,10},{10,1... | collective-permute-start | bytes 1769480 | tf_op jit(solution)/shard_map/ppermute | solution.py:62
  402.5 97.9 %collective-permute-start.5 = (bf16[2,32,24,192]{3,2,1,0:T(8,128)(2,1)}, bf16[2,32,24,192]{3,2,1,0:T(8,128)(2,1)}, u32[]{:S(2)}, u32[]{:S(2)}) collective-permute-start(bf16[2,32,24,192]{3,2,1,0:T(8,128)(2,1)} %collective-permute-done.3), channel_id=1, source_target_pairs={{0,7},{1,0},{2,1},{3,2},{4,3},{5,4},{6,5},{7,6},{8,15},{9,8},{10,9... | collective-permute-start | bytes 1769480 | tf_op jit(solution)/shard_map/ppermute | solution.py:65
  414.3 100.3 %collective-permute-start.6 = (bf16[2,32,24,192]{3,2,1,0:T(8,128)(2,1)}, bf16[2,32,24,192]{3,2,1,0:T(8,128)(2,1)}, u32[]{:S(2)}, u32[]{:S(2)}) collective-permute-start(bf16[2,32,24,192]{3,2,1,0:T(8,128)(2,1)} %collective-permute-done.4), channel_id=1, source_target_pairs={{0,1},{1,2},{2,3},{3,4},{4,5},{5,6},{6,7},{7,0},{8,9},{9,10},{10,1... | collective-permute-start | bytes 1769480 | tf_op jit(solution)/shard_map/ppermute | solution.py:62
  424.3 105.5 %all-to-all-start.2 = ((bf16[32,2,24]{2,1,0:T(2,128)(2,1)}), bf16[32,2,24]{2,1,0:T(2,128)(2,1)S(1)}, u32[]{:S(2)}, u32[]{:S(2)}) async-start(bf16[32,2,24]{2,1,0:T(2,128)(2,1)} %broadcast_select_fusion), calls=%async_computation.2 | async-start | bytes 32768 | tf_op jit(solution)/shard_map/all_to_all | solution.py:46
  528.4 11.5 %copy-start.4 = (s32[128,8]{0,1:T(8,128)S(1)}, s32[128,8]{0,1:T(8,128)}, u32[]{:S(2)}) copy-start(s32[128,8]{0,1:T(8,128)} %param.9) | copy-start | bytes 12292
  528.4 11.5 %copy-start.5 = (f32[128,8]{0,1:T(8,128)S(1)}, f32[128,8]{0,1:T(8,128)}, u32[]{:S(2)}) copy-start(f32[128,8]{0,1:T(8,128)} %param.10) | copy-start | bytes 12292
  529.8 45.1 %all-to-all-start.1 = ((bf16[2,32,24,512]{3,2,0,1:T(8,128)(2,1)}), bf16[2,32,24,512]{3,2,0,1:T(8,128)(2,1)}, u32[]{:S(2)}, u32[]{:S(2)}) async-start(bf16[2,32,24,512]{3,2,0,1:T(8,128)(2,1)} %copy.57), calls=%async_computation.1 | async-start | bytes 3145728 | tf_op jit(solution)/shard_map/all_to_all | solution.py:73
Sparse Core Ops, SparseCore 0:
  9.8 28.8 all-gather.1
